TPU v7x, 512 devices: a whole 4x4x16 slice. The times are simulated.
512 devices in a mesh: lat: 64 (over y, z), wid: 8 (over x, core).
Axes of the slice: x: 4, y: 4, z: 16, core: 2. Of those that a mesh axis runs over, the one named last changes fastest.
Arguments:
- activations: bfloat16 [128, 3584], P(None, 'wid'), may hold values from -6 to 6
- encoder: bfloat16 [3584, 32768], P('wid', 'lat'), may hold values from -0.09375 to 0.09375
- encoder_bias: float32 [32768], P('lat'), may hold values from -3 to 3
- decoder: bfloat16 [32768, 3584], P('lat', 'wid'), may hold values from -0.75 to 0.75
- decoder_bias: float32 [3584], P('wid'), may hold values from -3 to 3
- kept_mask: int32 [128, 32768], P(None, 'lat'), may hold values 0 or 1
- boundaries: int32 [8], replicated, may hold values from 4097 to 32768, as said below
Outputs:
- encoder_grad: bfloat16 [3584, 32768], P('wid', 'lat')
- encoder_bias_grad: float32 [32768], P('lat')
- decoder_grad: bfloat16 [32768, 3584], P('lat', 'wid')
- decoder_bias_grad: float32 [3584], P('wid')
Inputs may be any that keep to these rules, and one draw needn't show every extreme that they name: `boundaries`: Rising; for k below 7, boundary k lies among the 512 latents that follow (k + 1) * 4096; the last equals 32768.
All inputs are finite; a program needn't handle non-finite values. No bound on the sum of `kept_mask` on one device may be relied on, other than what follows from the above.
Results may differ from a plain program's by a relative error of at most 0.006.
Values may be sent and summed in bfloat16 or wider, within the bound.
No kernel may reach another device: no remote copies, remote signals or barrier semaphores. Data moves between devices by JAX's collectives and lax.ppermute only.
A program may use at most 128 MiB of HBM per device.

v0:
```python
import jax
import jax.numpy as jnp
from jax import lax
from jax.sharding import PartitionSpec as P

GROUPS = 8


def prefix(part, axis, combine, identity, reverse):
    count = lax.axis_size(axis)
    place = lax.axis_index(axis)
    ahead = count - 1 - place if reverse else place
    gathered = lax.all_gather(part, axis)
    state = jnp.zeros_like(part) + jnp.asarray(identity, part.dtype)

    def one(step, state):
        source = count - 1 - step if reverse else step
        return combine(state, lax.dynamic_index_in_dim(gathered, source, 0, False))

    return lax.fori_loop(0, ahead, one, state)


def add_terms(earlier, later):
    return earlier + later


def body(activations, encoder, encoder_bias, decoder, decoder_bias, kept_mask, boundaries):
    latent_width = encoder.shape[1]
    first_latent = lax.axis_index("lat") * latent_width
    latent_ids = first_latent + jnp.arange(latent_width, dtype=jnp.int32)
    kept_float = kept_mask.astype(jnp.float32)
    encoder_part = jnp.dot(activations, encoder, preferred_element_type=jnp.float32)
    preacts = lax.psum(encoder_part, "wid") + encoder_bias
    codes = (kept_float * preacts).astype(jnp.bfloat16)
    inside_rows = (boundaries > first_latent) & (boundaries <= first_latent + latent_width)
    holds_cut = jnp.any(inside_rows)
    cut_point = jnp.sum(jnp.where(inside_rows, boundaries, 0))
    below_cut = latent_ids < cut_point
    zero_code = jnp.zeros((), jnp.bfloat16)
    masked_codes = jnp.stack(
        [
            jnp.where(below_cut[None, :], codes, zero_code),
            jnp.where(below_cut[None, :], zero_code, codes),
        ]
    )
    decoded_pieces = jnp.einsum(
        "sbj,jd->sbd", masked_codes, decoder, preferred_element_type=jnp.float32
    )
    local_total = decoded_pieces[0] + decoded_pieces[1]
    zero_rows = jnp.zeros_like(local_total)
    prefix_sum = prefix(local_total, "lat", add_terms, zero_rows, False)
    target_rows = activations.astype(jnp.float32)
    scaled_error = jnp.where(
        holds_cut, (decoder_bias + prefix_sum + decoded_pieces[0] - target_rows) / GROUPS, 0.0
    )
    suffix_sum = prefix(scaled_error, "lat", add_terms, zero_rows, True)
    below_suffix = suffix_sum + scaled_error
    suffix_pair = jnp.stack([below_suffix, suffix_sum]).astype(jnp.bfloat16)
    back_grads = jnp.einsum("sbd,jd->sbj", suffix_pair, decoder, preferred_element_type=jnp.float32)
    partial_grads = jnp.where(below_cut[None, :], back_grads[0], back_grads[1])
    coded_grads = lax.psum(partial_grads, "wid")
    pre_grads = kept_float * coded_grads
    encoder_bias_grad = jnp.sum(pre_grads, axis=0)
    pre_low = pre_grads.astype(jnp.bfloat16)
    encoder_grad = lax.dot_general(
        activations, pre_low, (((0,), (0,)), ((), ())), preferred_element_type=jnp.float32
    ).astype(jnp.bfloat16)
    decoder_grad = jnp.einsum(
        "sbj,sbd->jd", masked_codes, suffix_pair, preferred_element_type=jnp.float32
    ).astype(jnp.bfloat16)
    decoder_bias_grad = lax.psum(jnp.sum(scaled_error, axis=0), "lat")
    return (encoder_grad, encoder_bias_grad, decoder_grad, decoder_bias_grad)


def solution(mesh):
    placed = (
        P(None, "wid"),
        P("wid", "lat"),
        P("lat"),
        P("lat", "wid"),
        P("wid"),
        P(None, "lat"),
        P(),
    )
    return jax.shard_map(
        body,
        mesh=mesh,
        in_specs=placed,
        out_specs=(P("wid", "lat"), P("lat"), P("lat", "wid"), P("wid")),
        check_vma=False,
    )
```

profile of v0, /device:TPU:32, one launch (start us, length us, event | category | flops | bytes accessed | tf_op | source)
XLA Modules:
  0.0 781.7 jit_solution(4494470858266741804)
XLA Ops:
  7.2 2.1 fusion.19
  9.4 1.3 select_reduce_fusion
  11.3 78.9 %all-reduce.3.cloned.1.call-done = f32[128,512]{1,0:T(8,128)} async-done(((f32[128,512]{1,0:T(8,128)}), f32[128,512]{1,0:T(8,128)}) %all-reduce.3.cloned.1.call-update) | async-done | bytes 262160 | tf_op jit(solution)/shard_map/psum | solution.py:33
  90.2 1.1 select_bitcast_fusion.1
  92.5 1.3 fusion.16
  93.8 180.1 %all-gather.4.cloned.1.call-done = f32[64,128,448]{1,2,0:T(8,128)} async-done(((f32[1,128,448]{1,2,0:T(8,128)}), f32[64,128,448]{1,2,0:T(8,128)}) %all-gather.4.cloned.1.call-update) | async-done | bytes 14680080 | tf_op jit(solution)/shard_map/all_gather | solution.py:13
  273.8 1.2 while.22
  275.2 2.4 fusion.17
  277.7 269.5 %all-gather.6.cloned.1.call-done = f32[8192,448]{0,1:T(8,128)} async-done(((f32[128,448]{0,1:T(8,128)}), f32[8192,448]{0,1:T(8,128)}) %all-gather.6.cloned.1.call-update) | async-done | bytes 14680080 | tf_op jit(solution)/shard_map/all_gather | solution.py:13
  547.1 16.6 %copy.25 = f32[8192,448]{1,0:T(8,128)} copy(f32[8192,448]{0,1:T(8,128)} %all-gather.6.cloned.1.call-done) | data formatting | bytes 29360128 | tf_op jit(solution)/shard_map/while | solution.py:20
  563.7 65.1 %while.23 = (s32[]{:T(128)}, f32[128,448]{1,0:T(8,128)S(1)}, s32[]{:T(128)}, f32[64,128,448]{2,1,0:T(8,128)}, s32[]{:T(128)}, /*index=5*/s32[]{:T(128)}, s32[]{:T(128)}, s32[]{:T(128)}) while((s32[]{:T(128)}, f32[128,448]{1,0:T(8,128)S(1)}, s32[]{:T(128)}, f32[64,128,448]{2,1,0:T(8,128)}, s32[]{:T(128)}, /*index=5*/s32[]{:T(128)}, s32[]{:T(128)}, ...), condition=%wide.region_6.7_spmd, body=%wide.region_5.6_spmd.sunk | while | flops 57350 | bytes 688263 | solution.py:20
  563.8 1.0 bitcast_add_fusion.6
  564.8 1.0 bitcast_add_fusion.6
  565.9 1.0 bitcast_add_fusion.6
  566.9 1.0 bitcast_add_fusion.6
  568.0 1.0 bitcast_add_fusion.6
  569.0 1.0 bitcast_add_fusion.6
  570.0 1.0 bitcast_add_fusion.6
  571.1 1.0 bitcast_add_fusion.6
  572.1 1.0 bitcast_add_fusion.6
  573.2 1.0 bitcast_add_fusion.6
  574.2 1.0 bitcast_add_fusion.6
  575.3 1.0 bitcast_add_fusion.6
  576.3 1.0 bitcast_add_fusion.6
  577.4 1.0 bitcast_add_fusion.6
  578.4 1.0 bitcast_add_fusion.6
  579.5 1.0 bitcast_add_fusion.6
  580.5 1.0 bitcast_add_fusion.6
  581.6 1.0 bitcast_add_fusion.6
  582.6 1.0 bitcast_add_fusion.6
  583.7 1.0 bitcast_add_fusion.6
  584.7 1.0 bitcast_add_fusion.6
  585.8 1.0 bitcast_add_fusion.6
  586.8 1.0 bitcast_add_fusion.6
  593.1 1.0 bitcast_add_fusion.6
  596.3 1.0 bitcast_add_fusion.6
  599.4 1.0 bitcast_add_fusion.6
  602.6 1.0 bitcast_add_fusion.6
  605.7 1.0 bitcast_add_fusion.6
  613.1 1.0 bitcast_add_fusion.6
  616.2 1.0 bitcast_add_fusion.6
  619.4 1.0 bitcast_add_fusion.6
  622.5 1.0 bitcast_add_fusion.6
  625.7 1.0 bitcast_add_fusion.6
  630.1 140.5 %psum.23 = f32[448]{0:T(512)} all-reduce(f32[448]{0:T(512)S(1)} %get-tuple-element.117), channel_id=1, replica_groups=mesh['lat'=64,'wid'=8] {'lat'}, use_global_device_ids=true, to_apply=%region_10.11 | all-reduce | flops 448 | bytes 3584 | tf_op jit(solution)/shard_map/psum | solution.py:71
  770.5 1.1 fusion
  771.6 2.0 fusion.1
  773.6 1.6 fusion.11
  (60 shorter events, 34.1 us)
Async XLA Ops:
  7.2 84.2 %copy-start = (bf16[512,448]{0,1:T(8,128)(2,1)S(1)}, bf16[512,448]{0,1:T(8,128)(2,1)}, u32[]{:S(2)}) copy-start(bf16[512,448]{0,1:T(8,128)(2,1)} %param.14) | copy-start | bytes 1376260
  7.2 83.0 %all-reduce.3.cloned.1.call-start = ((), (), s32[]{:S(2)}) async-start(), calls=%async_computation | async-start | bytes 524288 | tf_op jit(solution)/shard_map/psum | solution.py:33
  9.3 264.5 %all-gather.4.cloned.1.call-start = ((), (), s32[]{:S(2)}) async-start(), calls=%async_computation.1 | async-start | bytes 14909440 | tf_op jit(solution)/shard_map/all_gather | solution.py:13
  92.4 454.7 %all-gather.6.cloned.1.call-start = ((), (), s32[]{:S(2)}) async-start(), calls=%async_computation.3 | async-start | bytes 14909440 | tf_op jit(solution)/shard_map/all_gather | solution.py:13
  277.6 494.0 %all-reduce.5.cloned.1.call-start = ((), (), s32[]{:S(2)}) async-start(), calls=%async_computation.2 | async-start | bytes 524288 | tf_op jit(solution)/shard_map/psum | solution.py:61
  277.6 351.3 %copy-start.2 = (f32[128,448]{0,1:T(8,128)S(1)}, f32[128,448]{0,1:T(8,128)}, u32[]{:S(2)}) copy-start(f32[128,448]{0,1:T(8,128)} %get-tuple-element.118) | copy-start | bytes 688132
  277.6 494.0 %copy-start.1 = (s32[128,512]{1,0:T(8,128)S(1)}, s32[128,512]{1,0:T(8,128)}, u32[]{:S(2)}) copy-start(s32[128,512]{1,0:T(8,128)} %param.16) | copy-start | bytes 786436
  277.6 493.9 %copy-start.3 = (bf16[128,448]{0,1:T(8,128)(2,1)S(1)}, bf16[128,448]{0,1:T(8,128)(2,1)}, u32[]{:S(2)}) copy-start(bf16[128,448]{0,1:T(8,128)(2,1)} %param.11) | copy-start | bytes 344068
Sparse Core Ops, SparseCore 0:
  10.9 79.2 all-reduce.2
  94.2 179.6 all-gather.3
  277.7 269.3 all-gather.5
  630.2 65.3 all-reduce.4
where the time goes:
time: 784 us; the launch traced here: 782 us
  waiting for transfers between devices  528 us (67%)
  blocking collectives  140 us (18%)
  other arithmetic  73.2 us (9%)
  local copies, waits for them, and re-layouts  18 us (2%)
  between operations  13.9 us (2%)
    all_gather x2, waiting for transfers between devices, prefix(): gathered = lax.all_gather(part, axis)  450 us
    psum x1, blocking collectives, body(): decoder_bias_grad = lax.psum(jnp.sum(scaled_error, axis=0), 'lat')  140 us
    psum x1, waiting for transfers between devices, body(): preacts = lax.psum(encoder_part, 'wid') + encoder_bias  78.9 us
    add x63, other arithmetic, add_terms(): return earlier + later  63.4 us
    while x3, local copies, waits for them, and re-layouts, prefix(): return lax.fori_loop(0, ahead, one, state)  16.8 us
  transfers between devices with their start and end apart: 4, of which 3 were waited for; matrix products, arithmetic and copies ran while one was open for 1% of the time, Pallas kernels for 0%

commit v1 on v0

--- a/solution.py
+++ b/solution.py
@@ -30,7 +30,7 @@
     latent_ids = first_latent + jnp.arange(latent_width, dtype=jnp.int32)
     kept_float = kept_mask.astype(jnp.float32)
     encoder_part = jnp.dot(activations, encoder, preferred_element_type=jnp.float32)
-    preacts = lax.psum(encoder_part, "wid") + encoder_bias
+    preacts = jnp.sum(lax.all_gather(encoder_part, "wid"), axis=0) + encoder_bias
     codes = (kept_float * preacts).astype(jnp.bfloat16)
     inside_rows = (boundaries > first_latent) & (boundaries <= first_latent + latent_width)
     holds_cut = jnp.any(inside_rows)

time: 784 us -> 742 us (0.946)
  waiting for transfers between devices: 528 us -> 485 us
    psum x1 -> x0, waiting for transfers between devices: 78.9 us -> none  [body(): preacts = lax.psum(encoder_part, 'wid') + encoder_bias]
    all_gather x0 -> x1, waiting for transfers between devices: none -> 36.4 us  [body(): lax.all_gather(encoder_part, 'wid')]
where the time goes in v1:
time: 742 us; the launch traced here: 740 us
  waiting for transfers between devices  485 us (65%)
  blocking collectives  140 us (19%)
  other arithmetic  74.1 us (10%)
  local copies, waits for them, and re-layouts  18 us (2%)
  between operations  13.9 us (2%)
    all_gather x2, waiting for transfers between devices, prefix(): gathered = lax.all_gather(part, axis)  449 us
    psum x1, blocking collectives, body(): decoder_bias_grad = lax.psum(jnp.sum(scaled_error, axis=0), 'lat')  140 us
    add x63, other arithmetic, add_terms(): return earlier + later  63.4 us
    all_gather x1, waiting for transfers between devices, body(): lax.all_gather(encoder_part, 'wid')  36.4 us
    while x3, local copies, waits for them, and re-layouts, prefix(): return lax.fori_loop(0, ahead, one, state)  16.8 us
  transfers between devices with their start and end apart: 4, of which 3 were waited for; matrix products, arithmetic and copies ran while one was open for 1% of the time, Pallas kernels for 0%

profile of v1, /device:TPU:32, one launch (start us, length us, event | category | flops | bytes accessed | tf_op | source)
XLA Modules:
  0.0 739.6 jit_solution(13081505204496175749)
XLA Ops:
  7.2 2.1 fusion.19
  9.4 1.3 select_reduce_fusion
  11.4 36.4 %all-gather.8.cloned.1.call-done = f32[1024,512]{1,0:T(8,128)} async-done(((f32[128,512]{1,0:T(8,128)}), f32[1024,512]{1,0:T(8,128)}) %all-gather.8.cloned.1.call-update) | async-done | bytes 2097168 | tf_op jit(solution)/shard_map/all_gather | solution.py:33
  47.7 1.8 reduce_sum.37
  49.5 1.0 select_bitcast_fusion.1
  51.7 1.3 fusion.16
  53.0 179.6 %all-gather.6.cloned.1.call-done = f32[64,128,448]{1,2,0:T(8,128)} async-done(((f32[1,128,448]{1,2,0:T(8,128)}), f32[64,128,448]{1,2,0:T(8,128)}) %all-gather.6.cloned.1.call-update) | async-done | bytes 14680080 | tf_op jit(solution)/shard_map/all_gather | solution.py:13
  232.6 1.2 while.22
  234.0 1.5 fusion.17
  235.6 269.5 %all-gather.10.cloned.1.call-done = f32[8192,448]{0,1:T(8,128)} async-done(((f32[128,448]{0,1:T(8,128)}), f32[8192,448]{0,1:T(8,128)}) %all-gather.10.cloned.1.call-update) | async-done | bytes 14680080 | tf_op jit(solution)/shard_map/all_gather | solution.py:13
  505.0 16.6 %copy.25 = f32[8192,448]{1,0:T(8,128)} copy(f32[8192,448]{0,1:T(8,128)} %all-gather.10.cloned.1.call-done) | data formatting | bytes 29360128 | tf_op jit(solution)/shard_map/while | solution.py:20
  521.6 65.1 %while.23 = (s32[]{:T(128)}, f32[128,448]{1,0:T(8,128)S(1)}, s32[]{:T(128)}, f32[64,128,448]{2,1,0:T(8,128)}, s32[]{:T(128)}, /*index=5*/s32[]{:T(128)}, s32[]{:T(128)}, s32[]{:T(128)}) while((s32[]{:T(128)}, f32[128,448]{1,0:T(8,128)S(1)}, s32[]{:T(128)}, f32[64,128,448]{2,1,0:T(8,128)}, s32[]{:T(128)}, /*index=5*/s32[]{:T(128)}, s32[]{:T(128)}, ...), condition=%wide.region_6.7_spmd, body=%wide.region_5.6_spmd.sunk | while | flops 57350 | bytes 688263 | solution.py:20
  521.6 1.0 bitcast_add_fusion.6
  522.7 1.0 bitcast_add_fusion.6
  523.7 1.0 bitcast_add_fusion.6
  524.8 1.0 bitcast_add_fusion.6
  525.8 1.0 bitcast_add_fusion.6
  526.9 1.0 bitcast_add_fusion.6
  527.9 1.0 bitcast_add_fusion.6
  529.0 1.0 bitcast_add_fusion.6
  530.0 1.0 bitcast_add_fusion.6
  531.1 1.0 bitcast_add_fusion.6
  532.1 1.0 bitcast_add_fusion.6
  533.2 1.0 bitcast_add_fusion.6
  534.2 1.0 bitcast_add_fusion.6
  535.3 1.0 bitcast_add_fusion.6
  536.3 1.0 bitcast_add_fusion.6
  537.4 1.0 bitcast_add_fusion.6
  538.4 1.0 bitcast_add_fusion.6
  539.5 1.0 bitcast_add_fusion.6
  540.5 1.0 bitcast_add_fusion.6
  541.6 1.0 bitcast_add_fusion.6
  542.6 1.0 bitcast_add_fusion.6
  544.7 1.0 bitcast_add_fusion.6
  547.9 1.0 bitcast_add_fusion.6
  551.0 1.0 bitcast_add_fusion.6
  554.2 1.0 bitcast_add_fusion.6
  561.5 1.0 bitcast_add_fusion.6
  564.7 1.0 bitcast_add_fusion.6
  567.8 1.0 bitcast_add_fusion.6
  571.0 1.0 bitcast_add_fusion.6
  574.1 1.0 bitcast_add_fusion.6
  581.5 1.0 bitcast_add_fusion.6
  584.6 1.0 bitcast_add_fusion.6
  588.0 140.5 %psum.15 = f32[448]{0:T(512)} all-reduce(f32[448]{0:T(512)S(1)} %get-tuple-element.117), channel_id=1, replica_groups=mesh['lat'=64,'wid'=8] {'lat'}, use_global_device_ids=true, to_apply=%region_10.11 | all-reduce | flops 448 | bytes 3584 | tf_op jit(solution)/shard_map/psum | solution.py:71
  728.4 1.1 fusion
  729.5 2.0 fusion.1
  731.5 1.6 fusion.11
  (63 shorter events, 35.1 us)
Async XLA Ops:
  7.2 43.4 %copy-start = (bf16[512,448]{0,1:T(8,128)(2,1)S(1)}, bf16[512,448]{0,1:T(8,128)(2,1)}, u32[]{:S(2)}) copy-start(bf16[512,448]{0,1:T(8,128)(2,1)} %param.14) | copy-start | bytes 1376260
  7.2 226.8 %copy-start.3 = (bf16[128,448]{0,1:T(8,128)(2,1)S(1)}, bf16[128,448]{0,1:T(8,128)(2,1)}, u32[]{:S(2)}) copy-start(bf16[128,448]{0,1:T(8,128)(2,1)} %param.11) | copy-start | bytes 344068
  7.2 226.8 %copy-start.4 = (f32[448]{0:T(512)S(1)}, f32[448]{0:T(512)}, u32[]{:S(2)}) copy-start(f32[448]{0:T(512)} %param.15) | copy-start | bytes 5380
  7.2 40.5 %all-gather.8.cloned.1.call-start = ((), (), s32[]{:S(2)}) async-start(), calls=%async_computation.2 | async-start | bytes 2359296 | tf_op jit(solution)/shard_map/all_gather | solution.py:33
  9.3 223.3 %all-gather.6.cloned.1.call-start = ((), (), s32[]{:S(2)}) async-start(), calls=%async_computation | async-start | bytes 14909440 | tf_op jit(solution)/shard_map/all_gather | solution.py:13
  51.7 453.4 %all-gather.10.cloned.1.call-start = ((), (), s32[]{:S(2)}) async-start(), calls=%async_computation.3 | async-start | bytes 14909440 | tf_op jit(solution)/shard_map/all_gather | solution.py:13
  235.5 494.0 %all-reduce.2.cloned.1.call-start = ((), (), s32[]{:S(2)}) async-start(), calls=%async_computation.1 | async-start | bytes 524288 | tf_op jit(solution)/shard_map/psum | solution.py:61
  235.5 351.3 %copy-start.2 = (f32[128,448]{0,1:T(8,128)S(1)}, f32[128,448]{0,1:T(8,128)}, u32[]{:S(2)}) copy-start(f32[128,448]{0,1:T(8,128)} %get-tuple-element.118) | copy-start | bytes 688132
  235.6 493.9 %copy-start.1 = (s32[128,512]{1,0:T(8,128)S(1)}, s32[128,512]{1,0:T(8,128)}, u32[]{:S(2)}) copy-start(s32[128,512]{1,0:T(8,128)} %param.16) | copy-start | bytes 786436
Sparse Core Ops, SparseCore 0:
  10.8 36.9 all-gather.7
  51.8 180.7 all-gather.5
  236.1 268.8 all-gather.9
  588.1 65.3 all-reduce.1
